TPU v7x, 256 devices: a whole 4x4x8 slice. The times are simulated.
256 devices in a mesh: rep: 2 (over core), shard: 128 (over x, z, y).
Axes of the slice: x: 4, y: 4, z: 8, core: 2. Of those that a mesh axis runs over, the one named last changes fastest.
Arguments:
- grad: bfloat16 [192, 512, 2048], P(None, 'shard'), may hold values from -6 to 6
- momentum: bfloat16 [192, 512, 2048], P(None, 'shard'), may hold values from -6 to 6
- owners: int32 [2, 128, 2], replicated, may hold values from 0 to 192, as said below
Outputs:
- new_momentum: bfloat16 [192, 512, 2048], P(None, 'shard')
- update: bfloat16 [192, 512, 2048], P(None, 'shard')
Inputs may be any that keep to these rules, and one draw needn't show every extreme that they name: `owners`: no matrix index appears twice. In each device's row of 2 slots the entries naming matrices come before the empty ones (value 192). In every draw some device has all 2 slots filled, and some matrices are named by no slot.
All inputs are finite; a program needn't handle non-finite values.
Results may differ from a plain program's by a relative error of at most 0.013.
Values may be sent and summed in bfloat16 or wider, within the bound.
A program may use at most 128 MiB of HBM per device.

v0:
```python
import math

import jax
import jax.numpy as jnp
from jax import lax
from jax.sharding import PartitionSpec as P

R = 512
C = 2048
ITERS = 3


coef_a = 3.4445
coef_b = -4.775
coef_c = 2.0315
mom_decay = 0.95


def newton_schulz(matrix):
    whole = matrix.astype(jnp.float32)
    norm_value = jnp.sqrt(jnp.sum(whole * whole))
    current = (whole / (norm_value + 1e-07)).astype(jnp.bfloat16)
    scaled = None
    for turn_index in range(ITERS):
        gram = lax.dot_general(
            current, current, (((1,), (1,)), ((), ())), preferred_element_type=jnp.float32
        ).astype(jnp.bfloat16)
        square = jnp.dot(gram, gram, preferred_element_type=jnp.float32)
        mixer = (coef_b * gram.astype(jnp.float32) + coef_c * square).astype(jnp.bfloat16)
        result = coef_a * current.astype(jnp.float32) + jnp.dot(
            mixer, current, preferred_element_type=jnp.float32
        )
        if turn_index + 1 < ITERS:
            current = result.astype(jnp.bfloat16)
        else:
            scaled = (0.2 * math.sqrt(max(R, C)) * result).astype(jnp.bfloat16)
    return scaled


def spread_lists(owners, matrix_count, replicas, shard_count):
    devices = replicas * shard_count
    entries = owners.reshape(-1)
    alive = entries < matrix_count
    ordinal = jnp.cumsum(alive.astype(jnp.int32)) - 1
    per_device = (matrix_count + devices - 1) // devices
    target = jnp.where(alive, ordinal, devices * per_device)
    packed = (
        jnp.full((devices * per_device + 1,), matrix_count, jnp.int32)
        .at[target]
        .set(entries)[: devices * per_device]
    )
    return packed.reshape(per_device, shard_count, replicas).transpose(2, 1, 0)


def place_rows(returned, chosen, matrix_count):
    local_rows = returned.shape[1] // chosen.shape[1]
    pieces = returned.reshape(chosen.shape[0] * chosen.shape[1], local_rows, returned.shape[2])
    target = chosen.reshape(-1)
    empty = jnp.zeros((matrix_count, local_rows, returned.shape[2]), jnp.bfloat16)
    return empty.at[target].set(pieces, mode="drop")


def body(grad, momentum, owners):
    fresh = mom_decay * momentum.astype(jnp.float32) + grad.astype(jnp.float32)
    new_momentum = fresh.astype(jnp.bfloat16)
    nesterov = (grad.astype(jnp.float32) + mom_decay * fresh).astype(jnp.bfloat16)
    matrix_count = grad.shape[0]
    local_rows = grad.shape[1]
    width = grad.shape[2]
    replicas = lax.axis_size("rep")
    shard_count = lax.axis_size("shard")
    my_rep = lax.axis_index("rep")
    table = spread_lists(owners, matrix_count, replicas, shard_count)
    slot_count = table.shape[2]
    mine = lax.dynamic_index_in_dim(table, my_rep, 0, keepdims=False)
    chosen = mine.T
    usable = chosen < matrix_count
    taken = jnp.take(nesterov, jnp.minimum(chosen, matrix_count - 1), axis=0)
    outgoing = jnp.where(usable[:, :, None, None], taken, jnp.zeros_like(taken))
    outgoing = outgoing.reshape(slot_count, shard_count * local_rows, width)
    finished = lax.map(
        newton_schulz, lax.all_to_all(outgoing, "shard", split_axis=1, concat_axis=1, tiled=True)
    )
    returned = lax.all_to_all(finished, "shard", split_axis=1, concat_axis=1, tiled=True)
    both = lax.all_gather(returned, "rep", axis=0, tiled=True)
    every_choice = table.transpose(0, 2, 1).reshape(replicas * slot_count, shard_count)
    update = place_rows(both, every_choice, matrix_count)
    return (new_momentum, update)


def solution(mesh):
    placed = (P(None, "shard", None), P(None, "shard", None), P())
    return jax.shard_map(
        body,
        mesh=mesh,
        in_specs=placed,
        out_specs=(P(None, "shard", None), P(None, "shard", None)),
        check_vma=False,
    )
```

profile of v0, /device:TPU:19, one launch (start us, length us, event | category | flops | bytes accessed | tf_op | source)
XLA Modules:
  0.0 296.3 jit_solution(2510085038544679176)
XLA Ops:
  7.2 0.0 all-gather.2.cloned.1.call-start
  7.2 0.7 fusion.27
  7.9 0.8 copy.21
  8.7 0.1 copy.20
  8.9 0.1 reshape.208
  9.0 0.3 reduce-window.9
  9.3 0.1 slice.10
  9.4 0.1 slice_reduce_fusion
  9.5 0.1 add_add_fusion
  9.6 0.2 copy.19
  9.8 0.2 lt.81
  10.0 0.1 reshape.221
  10.1 2.4 scatter_custom_fusion
  12.6 0.1 reshape.206
  12.7 0.2 fusion.18
  12.9 0.2 compare_reduce_fusion
  13.1 7.1 %fusion = (bf16[192,4,2048]{2,1,0:T(4,128)(2,1)S(1)}, bf16[192,4,2048]{2,1,0:T(4,128)(2,1)}) fusion(bf16[192,4,2048]{2,1,0:T(4,128)(2,1)} %param.3, bf16[192,4,2048]{2,1,0:T(4,128)(2,1)} %param.4), kind=kLoop, calls=%fused_computation.5 | loop fusion | flops 12582912 | bytes 12582912 | tf_op jit(solution)/shard_map/convert_element_type | solution.py:66
  20.2 3.5 %gather_fusion = bf16[128,4,2048]{2,1,0:T(4,128)(2,1)} fusion(bf16[192,4,2048]{2,1,0:T(4,128)(2,1)S(1)} %get-tuple-element.15, s32[1024]{0:T(1024)S(1)} %pad_clamp_fusion), kind=kCustom, calls=%fused_computation | custom fusion | bytes 4194816 | tf_op jit(solution)/shard_map/jit(_take)/gather | solution.py:78
  23.7 2.5 gather.7
  26.3 0.1 broadcast_in_dim.51
  26.4 0.1 broadcast_in_dim.52
  26.5 0.1 broadcast_in_dim.54
  26.6 0.1 broadcast_in_dim.55
  26.7 0.3 select_select_fusion
  27.0 5.2 %copy.32 = bf16[1,512,2048]{2,0,1:T(2,128)(2,1)} copy(bf16[1,512,2048]{2,1,0:T(8,128)(2,1)S(1)} %select_select_fusion) | data formatting | bytes 4194304 | tf_op jit(solution)/shard_map/jit(_where)/select_n | solution.py:79
  32.2 0.5 broadcast.218
  32.7 13.1 %reduce.9 = bf16[512,2048]{1,0:T(8,128)(2,1)S(1)} reduce(bf16[512,1,2048]{2,1,0:T(2,128)(2,1)} %bitcast.34, bf16[]{:T(256)} %broadcast.218), dimensions={1}, to_apply=%bitcast.31.reduce_sub_computation | reduce | bytes 4194306
  45.8 2.8 reshape.240
  48.7 63.4 %all_to_all.10 = bf16[128,2,4096]{2,1,0:T(2,128)(2,1)S(1)} all-to-all(bf16[128,2,4096]{2,1,0:T(2,128)(2,1)} %reshape.240), channel_id=1, replica_groups=mesh['rep'=2,'shard'=128] {'shard'}, dimensions={0} | all-to-all | bytes 4194304 | tf_op jit(solution)/shard_map/all_to_all | solution.py:82
  112.0 6.8 %reshape.241 = bf16[512,1,2048]{2,1,0:T(2,128)(2,1)} reshape(bf16[128,2,4096]{2,1,0:T(2,128)(2,1)S(1)} %all_to_all.10) | data formatting | bytes 4194304
  118.8 4.8 %fusion.2 = f32[]{:T(128)} fusion(bf16[1,512,2048]{2,0,1:T(2,128)(2,1)} %bitcast.32), kind=kLoop, calls=%fused_computation.9 | loop fusion | flops 3145727 | bytes 2097156 | tf_op jit(solution)/shard_map/while/body/eval_jaxpr/reduce_sum | solution.py:21
  124.2 3.8 %fusion.5 = bf16[512,2048]{1,0:T(8,128)(2,1)S(1)} fusion(f32[]{:T(128)S(6)} %add.96, bf16[1,512,2048]{2,0,1:T(2,128)(2,1)} %bitcast.33), kind=kLoop, calls=%fused_computation.15 | loop fusion | flops 3145728 | bytes 4194308 | tf_op jit(solution)/shard_map/while/body/eval_jaxpr/convert_element_type | solution.py:22
  128.1 1.3 convolution_convert_fusion.2
  129.4 2.9 add_convert_fusion.1
  132.2 0.0 copy-start.1
  132.2 3.6 %convolution_convert_fusion.1 = bf16[512,512]{1,0:T(8,128)(2,1)S(1)} fusion(bf16[512,2048]{1,0:T(8,128)(2,1)} %add_convert_fusion.1), kind=kOutput, calls=%fused_computation.27 | convolution fusion | flops 1074003968 | bytes 2621440 | tf_op jit(solution)/shard_map/while/body/eval_jaxpr/dot_general | solution.py:25
  135.9 0.0 copy-done.1
  135.9 2.9 add_convert_fusion
  138.8 3.5 %convolution_convert_fusion = bf16[512,512]{1,0:T(8,128)(2,1)S(1)} fusion(bf16[512,2048]{1,0:T(8,128)(2,1)} %add_convert_fusion), kind=kOutput, calls=%fused_computation.26 | convolution fusion | flops 1074003968 | bytes 2621440 | tf_op jit(solution)/shard_map/while/body/eval_jaxpr/dot_general | solution.py:25
  142.3 3.8 %fusion.4 = bf16[1,512,2048]{2,1,0:T(8,128)(2,1)S(1)} fusion(bf16[512,2048]{1,0:T(8,128)(2,1)} %add_convert_fusion, bf16[512,512]{1,0:T(8,128)(2,1)S(1)} %convolution_convert_fusion), kind=kOutput, calls=%fused_computation.14 | convolution fusion | flops 1348730880 | bytes 4718592 | tf_op jit(solution)/shard_map/while/body/eval_jaxpr/dot_general | solution.py:30
  146.1 5.4 %copy.31 = bf16[1,512,2048]{2,0,1:T(2,128)(2,1)} copy(bf16[1,512,2048]{2,1,0:T(8,128)(2,1)S(1)} %fusion.4) | data formatting | bytes 4194304 | tf_op jit(solution)/shard_map/while/body/jit(dynamic_update_index_in_dim)/broadcast_in_dim | solution.py:81
  151.5 13.1 %reduce.10 = bf16[512,2048]{1,0:T(8,128)(2,1)S(1)} reduce(bf16[512,1,2048]{2,1,0:T(2,128)(2,1)} %bitcast.35, bf16[]{:T(256)} %broadcast.218), dimensions={1}, to_apply=%bitcast.30.reduce_sub_computation | reduce | bytes 4194306
  164.6 2.8 reshape.242
  167.4 59.1 %all_to_all.11 = bf16[128,2,4096]{2,1,0:T(2,128)(2,1)S(1)} all-to-all(bf16[128,2,4096]{2,1,0:T(2,128)(2,1)} %reshape.242), channel_id=1, replica_groups=mesh['rep'=2,'shard'=128] {'shard'}, dimensions={0} | all-to-all | bytes 4194304 | tf_op jit(solution)/shard_map/all_to_all | solution.py:84
  226.6 6.8 %reshape.243 = bf16[512,1,2048]{2,1,0:T(2,128)(2,1)} reshape(bf16[128,2,4096]{2,1,0:T(2,128)(2,1)S(1)} %all_to_all.11) | data formatting | bytes 4194304
  233.3 4.8 %copy.26 = bf16[1,512,2048]{2,1,0:T(8,128)(2,1)} copy(bf16[1,512,2048]{2,0,1:T(2,128)(2,1)} %bitcast.36) | data formatting | bytes 4194304 | tf_op jit(solution)/shard_map/all_to_all | solution.py:84
  238.1 0.0 all-gather.2.cloned.1.call-update
  238.2 0.1 copy.22
  238.2 18.5 %all-gather.2.cloned.1.call-done = bf16[2,512,2048]{2,1,0:T(8,128)(2,1)} async-done(((bf16[1,512,2048]{2,1,0:T(8,128)(2,1)}), bf16[2,512,2048]{2,1,0:T(8,128)(2,1)}) %all-gather.2.cloned.1.call-update) | async-done | bytes 4194320 | tf_op jit(solution)/shard_map/all_gather | solution.py:85
  256.7 7.2 %reshape.229 = bf16[256,4,2048]{2,1,0:T(4,128)(2,1)} reshape(bf16[2,512,2048]{2,1,0:T(8,128)(2,1)} %all-gather.2.cloned.1.call-done) | data formatting | bytes 8388608 | tf_op jit(solution)/shard_map/reshape | solution.py:57
  263.9 1.6 broadcast_in_dim.48
  265.5 22.2 %scatter_fusion = bf16[192,4,2048]{2,1,0:T(4,128)(2,1)S(1)} fusion(bf16[192,4,2048]{2,1,0:T(4,128)(2,1)S(1)} %broadcast_in_dim.48, s32[256]{0:T(256)S(1)} %bitcast.39, bf16[256,4,2048]{2,1,0:T(4,128)(2,1)} %reshape.229), kind=kCustom, calls=%fused_computation.2 | custom fusion | bytes 12583936 | tf_op jit(solution)/shard_map/scatter | solution.py:60
  287.7 0.0 copy-start
  287.8 1.7 copy-done
  (5 shorter events, 0.1 us)
Async XLA Ops:
  7.2 249.6 %all-gather.2.cloned.1.call-start = ((), (), s32[]{:S(2)}) async-start(), calls=%async_computation.2 | async-start | bytes 6291456 | tf_op jit(solution)/shard_map/all_gather | solution.py:85
  132.2 3.7 %copy-start.1 = (bf16[512,2048]{1,0:T(8,128)(2,1)S(1)}, bf16[512,2048]{1,0:T(8,128)(2,1)}, u32[]{:S(2)}) copy-start(bf16[512,2048]{1,0:T(8,128)(2,1)} %add_convert_fusion.1) | copy-start | bytes 6291460
  287.7 1.7 copy-start
Sparse Core Ops, SparseCore 0:
  238.3 18.4 all-gather.1
where the time goes:
time: 299 us; the launch traced here: 296 us
  blocking collectives  122 us (41%)
  local copies, waits for them, and re-layouts  78.6 us (26%)
  other arithmetic  43.7 us (15%)
  waiting for transfers between devices  18.5 us (6%)
  matrix products  18 us (6%)
  between operations  14.9 us (5%)
    all_to_all x1, blocking collectives, body(): lax.all_to_all(outgoing, 'shard', split_axis=1, concat_axis=1, tiled=True)  63.4 us
    all_to_all x1, blocking collectives, body(): lax.all_to_all(finished, 'shard', split_axis=1, concat_axis=1, tiled=True)  59.1 us
    unnamed x2, other arithmetic  26.2 us
    scatter x1, local copies, waits for them, and re-layouts, place_rows(): return empty.at[target].set(pieces, mode='drop')  22.2 us
    unnamed x10, local copies, waits for them, and re-layouts  22.2 us
    all_gather x1, waiting for transfers between devices, body(): both = lax.all_gather(returned, 'rep', axis=0, tiled=True)  18.5 us
    dot_general x3, matrix products, newton_schulz(): jnp.dot(mixer, current, preferred_element_type=jnp.float32)  9.57 us
    dot_general x3, matrix products, newton_schulz(): lax.dot_general(current, current, (((1,), (1,)), ((), ())), preferred_ele...  8.43 us
  transfers between devices with their start and end apart: 1, of which 1 were waited for; matrix products, arithmetic and copies ran while one was open for 0% of the time, Pallas kernels for 0%

commit v1 on v0

v1 whole, which is shorter than its diff:
```python
import math

import jax
import jax.numpy as jnp
from jax import lax
from jax.experimental import pallas as pl
from jax.experimental.pallas import tpu as pltpu
from jax.sharding import PartitionSpec as P

R = 512
C = 2048
ITERS = 3
MATS = 192

NX, NZ, NY = 4, 8, 4
CHIPS = NX * NZ * NY
PER_REP = MATS // 2
LANES = 128
COLS = C // LANES
ROWS = R // CHIPS
QUAD = 4
GROUPS = 8
PER_GROUP = CHIPS // GROUPS

coef_a = 3.4445
coef_b = -4.775
coef_c = 2.0315
mom_decay = 0.95
out_scale = 0.2 * math.sqrt(max(R, C))


def coords(chip):
    return chip // (NZ * NY), (chip // NY) % NZ, chip % NY


def phase(chip, rep):
    x, z, y = coords(chip)
    return (x + z + y + 2 * rep) % NY


def matrix_of(chip, rep):
    return PER_REP * rep + 3 * (chip // NY) + phase(chip, rep) - 1


def owner_of(slot, rep):
    row = slot // 3
    y = (slot % 3 + 1 + 2 * NY - (row // NZ + row % NZ + 2 * rep) % NY) % NY
    return row * NY + y


def offset(k):
    pair = k // NY
    return pair // NZ, (3 * pair) % NZ, k % NY


def dot(a, b, contract_b):
    return lax.dot_general(a, b, (((1,), (contract_b,)), ((), ())), preferred_element_type=jnp.float32)


def tile(row, col):
    return pl.ds(pl.multiple_of(row * 16, 16), 16), slice(col * LANES, (col + 1) * LANES)


def kernel(src, ret, xbuf, ybuf, xs, send1, recv1, send2, recv2, send3, recv3):
    me = lax.axis_index("shard")
    rep = lax.axis_index("rep")
    x, z, y = coords(me)
    mine = matrix_of(me, rep)
    active = phase(me, rep) != 0

    barrier = pltpu.get_barrier_semaphore()

    def greet(k, _):
        pl.semaphore_signal(barrier, 1, device_id={"shard": (me + k) % CHIPS})
        return 0

    lax.fori_loop(1, CHIPS, greet, 0)
    pl.semaphore_signal(barrier, 1, device_id={"rep": 1 - rep})
    pl.semaphore_wait(barrier, CHIPS)

    def spread(slot, _):
        dst = owner_of(slot, rep)
        matrix = PER_REP * rep + slot

        @pl.when(dst != me)
        def _():
            pltpu.make_async_remote_copy(
                src.at[matrix],
                xbuf.at[me // QUAD, :, me % QUAD],
                send1,
                recv1,
                device_id={"shard": dst},
            ).start()

        return 0

    lax.fori_loop(0, PER_REP, spread, 0)

    @pl.when(active)
    def _():
        pltpu.make_async_copy(src.at[mine], xbuf.at[me // QUAD, :, me % QUAD], recv1).start()
        pltpu.make_async_copy(xbuf, xbuf, recv1).wait()

        def gather(row, total):
            for col in range(COLS):
                part = xbuf[row, col].reshape(16, LANES)
                rows, lanes = tile(row, col)
                xs[rows, lanes] = part
                wide = part.astype(jnp.float32)
                total = total + wide * wide
            return total

        total = lax.fori_loop(0, R // 16, gather, jnp.zeros((16, LANES), jnp.float32))
        inverse = 1.0 / (jnp.sqrt(jnp.sum(total)) + 1e-07)
        current = (xs[...].astype(jnp.float32) * inverse).astype(jnp.bfloat16)
        for turn in range(ITERS):
            gram = dot(current, current, 1).astype(jnp.bfloat16)
            mixer = (coef_b * gram.astype(jnp.float32) + coef_c * dot(gram, gram, 0)).astype(jnp.bfloat16)
            result = coef_a * current.astype(jnp.float32) + dot(mixer, current, 0)
            if turn + 1 < ITERS:
                current = result.astype(jnp.bfloat16)
            else:
                xs[...] = (out_scale * result).astype(jnp.bfloat16)

        def scatter(row, _):
            for col in range(COLS):
                rows, lanes = tile(row, col)
                ybuf[row, col] = xs[rows, lanes].reshape(QUAD, ROWS, LANES)
            return 0

        lax.fori_loop(0, R // 16, scatter, 0)

        pltpu.make_async_copy(ybuf.at[me // QUAD, :, me % QUAD], ret.at[mine], recv2.at[0]).start()

        def back(k, _):
            dx, dz, dy = offset(k)
            dst = ((x + dx) % NX * NZ + (z + dz) % NZ) * NY + (y + dy) % NY
            pltpu.make_async_remote_copy(
                ybuf.at[dst // QUAD, :, dst % QUAD],
                ret.at[mine],
                send2,
                recv2.at[k // PER_GROUP],
                device_id={"shard": dst},
            ).start()
            return 0

        lax.fori_loop(1, CHIPS, back, 0)

    def collect(group, _):
        count = PER_GROUP * 3 // NY
        pltpu.make_async_copy(ret.at[pl.ds(0, count)], ret.at[pl.ds(0, count)], recv2.at[group]).wait()

        def forward(j, _):
            dx, dz, dy = offset(group * PER_GROUP + j)
            origin = ((x + NX - dx) % NX * NZ + (z + NZ - dz) % NZ) * NY + (y + NY - dy) % NY

            @pl.when(phase(origin, rep) != 0)
            def _():
                matrix = matrix_of(origin, rep)
                pltpu.make_async_remote_copy(
                    ret.at[matrix], ret.at[matrix], send3, recv3, device_id={"rep": 1 - rep}
                ).start()

            return 0

        lax.fori_loop(0, PER_GROUP, forward, 0)
        return 0

    lax.fori_loop(0, GROUPS, collect, 0)

    half = ret.at[pl.ds(0, PER_REP)]
    pltpu.make_async_copy(half, half, send3).wait()
    pltpu.make_async_copy(half, half, recv3).wait()

    @pl.when(active)
    def _():
        most = ret.at[pl.ds(0, PER_REP - 1)]
        pltpu.make_async_copy(most, most, send1).wait()
        rest = ret.at[pl.ds(0, CHIPS - 1)]
        pltpu.make_async_copy(rest, rest, send2).wait()

    @pl.when(jnp.logical_not(active))
    def _():
        pltpu.make_async_copy(half, half, send1).wait()


def exchange(nesterov):
    return pl.pallas_call(
        kernel,
        out_shape=jax.ShapeDtypeStruct((MATS, COLS, ROWS, LANES), jnp.bfloat16),
        in_specs=[pl.BlockSpec(memory_space=pl.ANY)],
        out_specs=pl.BlockSpec(memory_space=pl.ANY),
        scratch_shapes=[
            pltpu.VMEM((R // 16, COLS, QUAD, ROWS, LANES), jnp.bfloat16),
            pltpu.VMEM((R // 16, COLS, QUAD, ROWS, LANES), jnp.bfloat16),
            pltpu.VMEM((R, C), jnp.bfloat16),
            pltpu.SemaphoreType.DMA(()),
            pltpu.SemaphoreType.DMA(()),
            pltpu.SemaphoreType.DMA(()),
            pltpu.SemaphoreType.DMA((GROUPS,)),
            pltpu.SemaphoreType.DMA(()),
            pltpu.SemaphoreType.DMA(()),
        ],
        name="orthogonalize",
        compiler_params=pltpu.CompilerParams(
            collective_id=0, has_side_effects=True, vmem_limit_bytes=48 * 1024 * 1024
        ),
    )(nesterov)


def body(grad, momentum, owners):
    fresh = mom_decay * momentum.astype(jnp.float32) + grad.astype(jnp.float32)
    new_momentum = fresh.astype(jnp.bfloat16)
    nesterov = (grad.astype(jnp.float32) + mom_decay * fresh).astype(jnp.bfloat16)
    listed = jnp.any(owners.reshape(-1)[None, :] == jnp.arange(MATS, dtype=jnp.int32)[:, None], axis=1)
    blocks = nesterov.reshape(MATS, ROWS, COLS, LANES).transpose(0, 2, 1, 3)
    finished = exchange(blocks).transpose(0, 2, 1, 3).reshape(MATS, ROWS, C)
    update = jnp.where(listed[:, None, None], finished, jnp.zeros_like(finished))
    return (new_momentum, update)


def solution(mesh):
    placed = (P(None, "shard", None), P(None, "shard", None), P())
    return jax.shard_map(
        body,
        mesh=mesh,
        in_specs=placed,
        out_specs=(P(None, "shard", None), P(None, "shard", None)),
        check_vma=False,
    )
```

time: 299 us -> 131 us (0.44)
  the two profiles are of different devices: /device:TPU:19 before, /device:TPU:5 now
where the time goes in v1:
time: 131 us
  Pallas kernels  118 us (90%)
  other arithmetic  11.2 us (9%)
    pallas_call x1, Pallas kernels, exchange(): pl.pallas_call(kernel, out_shape=jax.ShapeDtypeStruct((MATS, COLS, ROWS,...  118 us
    transpose x1, other arithmetic, body(): blocks = nesterov.reshape(MATS, ROWS, COLS, LANES).transpose(0, 2, 1, 3)  7.94 us
    select_n x1, other arithmetic, body(): jnp.where(listed[:, None, None], finished, jnp.zeros_like(finished))  3.12 us

profile of v1, /device:TPU:5, one launch (start us, length us, event | category | flops | bytes accessed | tf_op | source)
XLA Modules:
  0.0 131.3 jit_solution(7078085394909655355)
XLA Ops:
  0.6 0.8 copy.6
  1.4 0.1 eq.15
  1.6 0.1 fusion.3
  1.7 7.9 %fusion.2 = (bf16[192,16,4,128]{3,2,1,0:T(4,128)(2,1)}, bf16[192,4,2048]{2,1,0:T(4,128)(2,1)}) fusion(bf16[192,4,2048]{2,1,0:T(4,128)(2,1)} %param.4, bf16[192,4,2048]{2,1,0:T(4,128)(2,1)} %param.3), kind=kLoop, calls=%fused_computation.4 | loop fusion | flops 12582912 | bytes 12582912 | tf_op jit(solution)/shard_map/transpose | solution.py:216
  9.7 118.5 %orthogonalize.1 = bf16[192,16,4,128]{3,2,1,0:T(4,128)(2,1)S(1)} custom-call(bf16[192,16,4,128]{3,2,1,0:T(4,128)(2,1)} %get-tuple-element.2.src), custom_call_target="tpu_custom_call" | custom-call | tf_op jit(solution)/shard_map/orthogonalize/pallas_call | solution.py:188
  128.1 3.1 %bitcast_select_fusion = bf16[192,4,2048]{2,1,0:T(4,128)(2,1)} fusion(bf16[192,16,4,128]{3,2,1,0:T(4,128)(2,1)S(1)} %orthogonalize.1, pred[192]{0:T(512)(128)(4,1)S(1)} %fusion.3), kind=kLoop, calls=%fused_computation.5 | loop fusion | flops 1572864 | bytes 6291648 | tf_op jit(solution)/shard_map/jit(_where)/select_n | solution.py:218

commit v2 on v1

--- a/solution.py
+++ b/solution.py
@@ -19,8 +19,6 @@
 COLS = C // LANES
 ROWS = R // CHIPS
 QUAD = 4
-GROUPS = 8
-PER_GROUP = CHIPS // GROUPS
 
 coef_a = 3.4445
 coef_b = -4.775
@@ -48,9 +46,12 @@
     return row * NY + y
 
 
-def offset(k):
-    pair = k // NY
-    return pair // NZ, (3 * pair) % NZ, k % NY
+def forth(k, chip):
+    return 3 * ((13 * (k % 32) + chip // NY) % 32) + k // 32
+
+
+def back_order(k):
+    return (37 * k) % CHIPS
 
 
 def dot(a, b, contract_b):
@@ -64,7 +65,6 @@
 def kernel(src, ret, xbuf, ybuf, xs, send1, recv1, send2, recv2, send3, recv3):
     me = lax.axis_index("shard")
     rep = lax.axis_index("rep")
-    x, z, y = coords(me)
     mine = matrix_of(me, rep)
     active = phase(me, rep) != 0
 
@@ -78,7 +78,8 @@
     pl.semaphore_signal(barrier, 1, device_id={"rep": 1 - rep})
     pl.semaphore_wait(barrier, CHIPS)
 
-    def spread(slot, _):
+    def spread(k, _):
+        slot = forth(k, me)
         dst = owner_of(slot, rep)
         matrix = PER_REP * rep + slot
 
@@ -130,47 +131,29 @@
 
         lax.fori_loop(0, R // 16, scatter, 0)
 
-        pltpu.make_async_copy(ybuf.at[me // QUAD, :, me % QUAD], ret.at[mine], recv2.at[0]).start()
-
         def back(k, _):
-            dx, dz, dy = offset(k)
-            dst = ((x + dx) % NX * NZ + (z + dz) % NZ) * NY + (y + dy) % NY
-            pltpu.make_async_remote_copy(
-                ybuf.at[dst // QUAD, :, dst % QUAD],
-                ret.at[mine],
-                send2,
-                recv2.at[k // PER_GROUP],
-                device_id={"shard": dst},
-            ).start()
+            dst = back_order(k)
+
+            @pl.when(dst != me)
+            def _():
+                pltpu.make_async_remote_copy(
+                    ybuf.at[dst // QUAD, :, dst % QUAD],
+                    ret.at[mine],
+                    send2,
+                    recv2,
+                    device_id={"shard": dst},
+                ).start()
+
             return 0
 
-        lax.fori_loop(1, CHIPS, back, 0)
-
-    def collect(group, _):
-        count = PER_GROUP * 3 // NY
-        pltpu.make_async_copy(ret.at[pl.ds(0, count)], ret.at[pl.ds(0, count)], recv2.at[group]).wait()
-
-        def forward(j, _):
-            dx, dz, dy = offset(group * PER_GROUP + j)
-            origin = ((x + NX - dx) % NX * NZ + (z + NZ - dz) % NZ) * NY + (y + NY - dy) % NY
-
-            @pl.when(phase(origin, rep) != 0)
-            def _():
-                matrix = matrix_of(origin, rep)
-                pltpu.make_async_remote_copy(
-                    ret.at[matrix], ret.at[matrix], send3, recv3, device_id={"rep": 1 - rep}
-                ).start()
-
-            return 0
-
-        lax.fori_loop(0, PER_GROUP, forward, 0)
-        return 0
-
-    lax.fori_loop(0, GROUPS, collect, 0)
-
-    half = ret.at[pl.ds(0, PER_REP)]
-    pltpu.make_async_copy(half, half, send3).wait()
-    pltpu.make_async_copy(half, half, recv3).wait()
+        lax.fori_loop(0, CHIPS, back, 0)
+        pltpu.make_async_copy(ybuf.at[me // QUAD, :, me % QUAD], ret.at[mine], recv2).start()
+
+    half = ret.at[pl.ds(PER_REP * rep, PER_REP)]
+    pltpu.make_async_copy(half, half, recv2).wait()
+    copy = pltpu.make_async_remote_copy(half, half, send3, recv3, device_id={"rep": 1 - rep})
+    copy.start()
+    copy.wait()
 
     @pl.when(active)
     def _():
@@ -197,7 +180,7 @@
             pltpu.SemaphoreType.DMA(()),
             pltpu.SemaphoreType.DMA(()),
             pltpu.SemaphoreType.DMA(()),
-            pltpu.SemaphoreType.DMA((GROUPS,)),
+            pltpu.SemaphoreType.DMA(()),
             pltpu.SemaphoreType.DMA(()),
             pltpu.SemaphoreType.DMA(()),
         ],

time: 131 us -> 105 us (0.80)
  the two profiles are of different devices: /device:TPU:5 before, /device:TPU:19 now
where the time goes in v2:
time: 105 us
  Pallas kernels  91.7 us (87%)
  other arithmetic  11.2 us (11%)
    pallas_call x1, Pallas kernels, exchange(): pl.pallas_call(kernel, out_shape=jax.ShapeDtypeStruct((MATS, COLS, ROWS,...  91.7 us
    transpose x1, other arithmetic, body(): blocks = nesterov.reshape(MATS, ROWS, COLS, LANES).transpose(0, 2, 1, 3)  7.94 us
    select_n x1, other arithmetic, body(): jnp.where(listed[:, None, None], finished, jnp.zeros_like(finished))  3.12 us

profile of v2, /device:TPU:19, one launch (start us, length us, event | category | flops | bytes accessed | tf_op | source)
XLA Modules:
  0.0 104.5 jit_solution(7040363673144844032)
XLA Ops:
  0.6 0.8 copy.6
  1.4 0.1 eq.15
  1.6 0.1 fusion.3
  1.7 7.9 %fusion.2 = (bf16[192,16,4,128]{3,2,1,0:T(4,128)(2,1)}, bf16[192,4,2048]{2,1,0:T(4,128)(2,1)}) fusion(bf16[192,4,2048]{2,1,0:T(4,128)(2,1)} %param.4, bf16[192,4,2048]{2,1,0:T(4,128)(2,1)} %param.3), kind=kLoop, calls=%fused_computation.4 | loop fusion | flops 12582912 | bytes 12582912 | tf_op jit(solution)/shard_map/transpose | solution.py:199
  9.7 91.7 %orthogonalize.1 = bf16[192,16,4,128]{3,2,1,0:T(4,128)(2,1)S(1)} custom-call(bf16[192,16,4,128]{3,2,1,0:T(4,128)(2,1)} %get-tuple-element.2.src), custom_call_target="tpu_custom_call" | custom-call | tf_op jit(solution)/shard_map/orthogonalize/pallas_call | solution.py:171
  101.4 3.1 %bitcast_select_fusion = bf16[192,4,2048]{2,1,0:T(4,128)(2,1)} fusion(bf16[192,16,4,128]{3,2,1,0:T(4,128)(2,1)S(1)} %orthogonalize.1, pred[192]{0:T(512)(128)(4,1)S(1)} %fusion.3), kind=kLoop, calls=%fused_computation.5 | loop fusion | flops 1572864 | bytes 6291648 | tf_op jit(solution)/shard_map/jit(_where)/select_n | solution.py:201

commit v3 on v2

v3 whole, which is shorter than its diff:
```python
import math

import jax
import jax.numpy as jnp
from jax import lax
from jax.experimental import pallas as pl
from jax.experimental.pallas import tpu as pltpu
from jax.sharding import PartitionSpec as P

R = 512
C = 2048
ITERS = 3
MATS = 192

NX, NZ, NY = 4, 8, 4
CHIPS = NX * NZ * NY
LINES = NX * NZ
PER_REP = MATS // 2
THIRDS = 3
LANES = 128
COLS = C // LANES
ROWS = R // CHIPS
QUAD = 16 // ROWS
CHUNKS = 4
CHUNK = PER_REP // CHUNKS

coef_a = 3.4445
coef_b = -4.775
coef_c = 2.0315
mom_decay = 0.95
out_scale = 0.2 * math.sqrt(max(R, C))


def line_phase(line, rep):
    return (line // NZ + line % NZ + 2 * rep) % NY


def phase(chip, rep):
    return (line_phase(chip // NY, rep) + chip % NY) % NY


def owner_of(third, line, rep):
    return line * NY + (third + 1 + NY - line_phase(line, rep)) % NY


def dot(a, b, contract_b):
    return lax.dot_general(a, b, (((1,), (contract_b,)), ((), ())), preferred_element_type=jnp.float32)


def tile(row, col):
    return pl.ds(pl.multiple_of(row * 16, 16), 16), slice(col * LANES, (col + 1) * LANES)


def kernel(
    grad, momentum, owners, fresh_out, update,
    gbuf, mbuf, fbuf, nbuf, xbuf, ybuf, xs,
    load_sem, store_sem, send1, recv1, send2, recv2, send3, recv3,
):
    me = lax.axis_index("shard")
    rep = lax.axis_index("rep")
    turn_of_me = phase(me, rep)
    active = turn_of_me != 0
    mine = PER_REP * rep + LINES * (turn_of_me - 1) + me // NY

    barrier = pltpu.get_barrier_semaphore()

    def load(part):
        first = jnp.where(part < CHUNKS, rep, 1 - rep) * PER_REP + part % CHUNKS * CHUNK
        where = pl.ds(first, CHUNK)
        return (
            pltpu.make_async_copy(grad.at[where], gbuf.at[where], load_sem.at[0, part]),
            pltpu.make_async_copy(momentum.at[where], mbuf.at[where], load_sem.at[1, part]),
        )

    def start_load(part, _):
        for copy in load(part):
            copy.start()
        return 0

    lax.fori_loop(0, 2 * CHUNKS, start_load, 0)

    def greet(k, _):
        pl.semaphore_signal(barrier, 1, device_id={"shard": (me + k) % CHIPS})
        return 0

    lax.fori_loop(1, CHIPS, greet, 0)
    pl.semaphore_signal(barrier, 1, device_id={"rep": 1 - rep})

    def combine(part, own):
        for copy in load(part):
            copy.wait()
        first = (rep if own else 1 - rep) * PER_REP + part % CHUNKS * CHUNK

        def one(i, _):
            for j in range(0, COLS, QUAD):
                g = gbuf[first + i, j : j + QUAD].reshape(16, LANES).astype(jnp.float32)
                m = mbuf[first + i, j : j + QUAD].reshape(16, LANES).astype(jnp.float32)
                fresh = mom_decay * m + g
                fbuf[first + i, j : j + QUAD] = fresh.astype(jnp.bfloat16).reshape(QUAD, ROWS, LANES)
                if own:
                    nesterov = (g + mom_decay * fresh).astype(jnp.bfloat16)
                    nbuf[part * CHUNK + i, j : j + QUAD] = nesterov.reshape(QUAD, ROWS, LANES)
            return 0

        lax.fori_loop(0, CHUNK, one, 0)

    def own_part(part, _):
        combine(part, True)
        return 0

    lax.fori_loop(0, CHUNKS, own_part, 0)
    pl.semaphore_wait(barrier, CHIPS)

    def spread(k, _):
        third = k // LINES
        line = (13 * (k % LINES) + me // NY) % LINES
        dst = owner_of(third, line, rep)

        @pl.when(dst != me)
        def _():
            pltpu.make_async_remote_copy(
                nbuf.at[LINES * third + line],
                xbuf.at[me // QUAD, :, me % QUAD],
                send1,
                recv1,
                device_id={"shard": dst},
            ).start()

        return 0

    lax.fori_loop(0, PER_REP, spread, 0)

    @pl.when(active)
    def _():
        pltpu.make_async_copy(
            nbuf.at[LINES * (turn_of_me - 1) + me // NY], xbuf.at[me // QUAD, :, me % QUAD], recv1
        ).start()

    def other_part(part, _):
        combine(part, False)
        return 0

    lax.fori_loop(CHUNKS, 2 * CHUNKS, other_part, 0)
    store = pltpu.make_async_copy(fbuf, fresh_out, store_sem)
    store.start()

    @pl.when(active)
    def _():
        pltpu.make_async_copy(xbuf, xbuf, recv1).wait()

        def gather(row, total):
            for col in range(COLS):
                part = xbuf[row, col].reshape(16, LANES)
                rows, lanes = tile(row, col)
                xs[rows, lanes] = part
                wide = part.astype(jnp.float32)
                total = total + wide * wide
            return total

        total = lax.fori_loop(0, R // 16, gather, jnp.zeros((16, LANES), jnp.float32))
        inverse = 1.0 / (jnp.sqrt(jnp.sum(total)) + 1e-07)
        current = (xs[...].astype(jnp.float32) * inverse).astype(jnp.bfloat16)
        listed = jnp.sum((owners[...] == mine).astype(jnp.int32)) > 0
        for turn in range(ITERS):
            gram = dot(current, current, 1).astype(jnp.bfloat16)
            mixer = (coef_b * gram.astype(jnp.float32) + coef_c * dot(gram, gram, 0)).astype(jnp.bfloat16)
            result = coef_a * current.astype(jnp.float32) + dot(mixer, current, 0)
            if turn + 1 < ITERS:
                current = result.astype(jnp.bfloat16)
            else:
                xs[...] = jnp.where(listed, out_scale * result, 0.0).astype(jnp.bfloat16)

        def scatter(row, _):
            for col in range(COLS):
                rows, lanes = tile(row, col)
                ybuf[row, col] = xs[rows, lanes].reshape(QUAD, ROWS, LANES)
            return 0

        lax.fori_loop(0, R // 16, scatter, 0)

        def back(k, _):
            dst = (37 * k) % CHIPS

            @pl.when(dst != me)
            def _():
                pltpu.make_async_remote_copy(
                    ybuf.at[dst // QUAD, :, dst % QUAD],
                    update.at[mine],
                    send2,
                    recv2.at[turn_of_me - 1],
                    device_id={"shard": dst},
                ).start()

            return 0

        lax.fori_loop(0, CHIPS, back, 0)
        pltpu.make_async_copy(
            ybuf.at[me // QUAD, :, me % QUAD], update.at[mine], recv2.at[turn_of_me - 1]
        ).start()

    def third_of(part):
        return update.at[pl.ds(PER_REP * rep + LINES * part, LINES)]

    def forward(part, _):
        pltpu.make_async_copy(third_of(part), third_of(part), recv2.at[part]).wait()
        pltpu.make_async_remote_copy(
            third_of(part), third_of(part), send3.at[part], recv3.at[part], device_id={"rep": 1 - rep}
        ).start()
        return 0

    lax.fori_loop(0, THIRDS, forward, 0)

    def finish(part, _):
        pltpu.make_async_copy(third_of(part), third_of(part), send3.at[part]).wait()
        pltpu.make_async_copy(third_of(part), third_of(part), recv3.at[part]).wait()
        return 0

    lax.fori_loop(0, THIRDS, finish, 0)
    store.wait()

    @pl.when(active)
    def _():
        most = nbuf.at[pl.ds(0, PER_REP - 1)]
        pltpu.make_async_copy(most, most, send1).wait()
        rest = update.at[pl.ds(0, CHIPS - 1)]
        pltpu.make_async_copy(rest, rest, send2).wait()

    @pl.when(jnp.logical_not(active))
    def _():
        pltpu.make_async_copy(nbuf, nbuf, send1).wait()


def whole(count):
    return jax.ShapeDtypeStruct((count, COLS, ROWS, LANES), jnp.bfloat16)


def buffer(*shape):
    return pltpu.VMEM(shape, jnp.bfloat16)


def step(grad, momentum, owners):
    dma = pltpu.SemaphoreType.DMA
    anywhere = pl.BlockSpec(memory_space=pl.ANY)
    in_hbm = pl.BlockSpec(memory_space=pltpu.MemorySpace.HBM)
    return pl.pallas_call(
        kernel,
        out_shape=(whole(MATS), whole(MATS)),
        in_specs=[in_hbm, in_hbm, pl.BlockSpec(memory_space=pltpu.VMEM)],
        out_specs=(anywhere, anywhere),
        scratch_shapes=[
            buffer(MATS, COLS, ROWS, LANES),
            buffer(MATS, COLS, ROWS, LANES),
            buffer(MATS, COLS, ROWS, LANES),
            buffer(PER_REP, COLS, ROWS, LANES),
            buffer(R // 16, COLS, QUAD, ROWS, LANES),
            buffer(R // 16, COLS, QUAD, ROWS, LANES),
            buffer(R, C),
            dma((2, 2 * CHUNKS)),
            dma(()),
            dma(()),
            dma(()),
            dma(()),
            dma((THIRDS,)),
            dma((THIRDS,)),
            dma((THIRDS,)),
        ],
        name="muon_step",
        compiler_params=pltpu.CompilerParams(
            collective_id=0, has_side_effects=True, vmem_limit_bytes=40 * 1024 * 1024
        ),
    )(grad, momentum, owners)


def body(grad, momentum, owners):
    def blocks(a):
        return a.reshape(MATS, ROWS, COLS, LANES).transpose(0, 2, 1, 3)

    def rows(a):
        return a.transpose(0, 2, 1, 3).reshape(MATS, ROWS, C)

    new_momentum, update = step(blocks(grad), blocks(momentum), owners.transpose(0, 2, 1))
    return (rows(new_momentum), rows(update))


def solution(mesh):
    placed = (P(None, "shard", None), P(None, "shard", None), P())
    return jax.shard_map(
        body,
        mesh=mesh,
        in_specs=placed,
        out_specs=(P(None, "shard", None), P(None, "shard", None)),
        check_vma=False,
    )
```

time: 105 us -> 102 us (0.971)
  other arithmetic: 11.2 us -> 0 us
  local copies, waits for them, and re-layouts: 0.95 us -> 7.78 us
  Pallas kernels: 91.7 us -> 93.6 us
    transpose x1 -> x0, other arithmetic: 7.94 us -> none  [body(): blocks = nesterov.reshape(MATS, ROWS, COLS, LANES).transpose(0, 2, 1, 3)]
    unnamed x1 -> x8, local copies, waits for them, and re-layouts: 0.81 us -> 7.78 us
    select_n x1 -> x0, other arithmetic: 3.12 us -> none  [body(): jnp.where(listed[:, None, None], finished, jnp.zeros_like(finished))]
    pallas_call x1, Pallas kernels: 91.7 us -> 93.6 us  [step(): pl.pallas_call(kernel, out_shape=(whole(MATS), whole(MATS)), in_specs=[in...]
where the time goes in v3:
time: 102 us
  Pallas kernels  93.6 us (92%)
  local copies, waits for them, and re-layouts  7.78 us (8%)
    pallas_call x1, Pallas kernels, step(): pl.pallas_call(kernel, out_shape=(whole(MATS), whole(MATS)), in_specs=[in...  93.6 us
    unnamed x8, local copies, waits for them, and re-layouts  7.78 us

profile of v3, /device:TPU:19, one launch (start us, length us, event | category | flops | bytes accessed | tf_op | source)
XLA Modules:
  0.0 102.0 jit_solution(2101976456758559918)
XLA Ops:
  0.6 0.0 copy-start
  0.6 1.9 %copy-done = bf16[192,4,2048]{2,1,0:T(4,128)(2,1)S(1)} copy-done((bf16[192,4,2048]{2,1,0:T(4,128)(2,1)S(1)}, bf16[192,4,2048]{2,1,0:T(4,128)(2,1)}, u32[]{:S(2)}) %copy-start) | copy-done | bytes 3145752
  2.5 0.0 copy-start.1
  2.5 1.9 %copy-done.1 = bf16[192,4,2048]{2,1,0:T(4,128)(2,1)S(1)} copy-done((bf16[192,4,2048]{2,1,0:T(4,128)(2,1)S(1)}, bf16[192,4,2048]{2,1,0:T(4,128)(2,1)}, u32[]{:S(2)}) %copy-start.1) | copy-done | bytes 3145752
  4.4 0.0 copy-start.2
  4.4 0.7 copy-done.2
  5.1 93.6 %muon_step.1 = (bf16[192,16,4,128]{3,2,1,0:T(4,128)(2,1)S(1)}, bf16[192,16,4,128]{3,2,1,0:T(4,128)(2,1)S(1)}) custom-call(bf16[192,16,4,128]{3,2,1,0:T(4,128)(2,1)S(1)} %bitcast.13, bf16[192,16,4,128]{3,2,1,0:T(4,128)(2,1)S(1)} %bitcast.14, s32[2,2,128]{2,1,0:T(2,128)S(1)} %bitcast.17), custom_call_target="tpu_custom_call" | custom-call | tf_op jit(solution)/shard_map/muon_step/pallas_call | solution.py:245
  98.7 1.7 %copy.7 = bf16[192,4,2048]{2,1,0:T(4,128)(2,1)} copy(bf16[192,4,2048]{2,1,0:T(4,128)(2,1)S(1)} %bitcast.16) | data formatting | bytes 6291456
  100.3 1.7 %copy.8 = bf16[192,4,2048]{2,1,0:T(4,128)(2,1)} copy(bf16[192,4,2048]{2,1,0:T(4,128)(2,1)S(1)} %bitcast.15) | data formatting | bytes 6291456
Async XLA Ops:
  0.6 1.9 %copy-start = (bf16[192,4,2048]{2,1,0:T(4,128)(2,1)S(1)}, bf16[192,4,2048]{2,1,0:T(4,128)(2,1)}, u32[]{:S(2)}) copy-start(bf16[192,4,2048]{2,1,0:T(4,128)(2,1)} %param.3) | copy-start | bytes 9437188
  2.5 1.9 %copy-start.1 = (bf16[192,4,2048]{2,1,0:T(4,128)(2,1)S(1)}, bf16[192,4,2048]{2,1,0:T(4,128)(2,1)}, u32[]{:S(2)}) copy-start(bf16[192,4,2048]{2,1,0:T(4,128)(2,1)} %param.4) | copy-start | bytes 9437188
  4.4 0.7 copy-start.2

commit v4 on v3

--- a/solution.py
+++ b/solution.py
@@ -53,8 +53,8 @@
 
 def kernel(
     grad, momentum, owners, fresh_out, update,
-    gbuf, mbuf, fbuf, nbuf, xbuf, ybuf, xs,
-    load_sem, store_sem, send1, recv1, send2, recv2, send3, recv3,
+    table, gbuf, mbuf, fbuf, nbuf, xbuf, ybuf, xs,
+    load_sem, table_sem, store_sem, send1, recv1, send2, recv2, send3, recv3,
 ):
     me = lax.axis_index("shard")
     rep = lax.axis_index("rep")
@@ -78,6 +78,8 @@
         return 0
 
     lax.fori_loop(0, 2 * CHUNKS, start_load, 0)
+    table_load = pltpu.make_async_copy(owners, table, table_sem)
+    table_load.start()
 
     def greet(k, _):
         pl.semaphore_signal(barrier, 1, device_id={"shard": (me + k) % CHIPS})
@@ -141,6 +143,7 @@
         return 0
 
     lax.fori_loop(CHUNKS, 2 * CHUNKS, other_part, 0)
+    table_load.wait()
     store = pltpu.make_async_copy(fbuf, fresh_out, store_sem)
     store.start()
 
@@ -160,7 +163,7 @@
         total = lax.fori_loop(0, R // 16, gather, jnp.zeros((16, LANES), jnp.float32))
         inverse = 1.0 / (jnp.sqrt(jnp.sum(total)) + 1e-07)
         current = (xs[...].astype(jnp.float32) * inverse).astype(jnp.bfloat16)
-        listed = jnp.sum((owners[...] == mine).astype(jnp.int32)) > 0
+        listed = jnp.sum((table[...] == mine).astype(jnp.int32)) > 0
         for turn in range(ITERS):
             gram = dot(current, current, 1).astype(jnp.bfloat16)
             mixer = (coef_b * gram.astype(jnp.float32) + coef_c * dot(gram, gram, 0)).astype(jnp.bfloat16)
@@ -179,7 +182,8 @@
         lax.fori_loop(0, R // 16, scatter, 0)
 
         def back(k, _):
-            dst = (37 * k) % CHIPS
+            x, z, y = me // (NZ * NY), me // NY % NZ, me % NY
+            dst = 37 * k % CHIPS
 
             @pl.when(dst != me)
             def _():
@@ -241,13 +245,13 @@
 def step(grad, momentum, owners):
     dma = pltpu.SemaphoreType.DMA
     anywhere = pl.BlockSpec(memory_space=pl.ANY)
-    in_hbm = pl.BlockSpec(memory_space=pltpu.MemorySpace.HBM)
     return pl.pallas_call(
         kernel,
         out_shape=(whole(MATS), whole(MATS)),
-        in_specs=[in_hbm, in_hbm, pl.BlockSpec(memory_space=pltpu.VMEM)],
+        in_specs=[anywhere, anywhere, anywhere],
         out_specs=(anywhere, anywhere),
         scratch_shapes=[
+            pltpu.VMEM((2, 2, CHIPS), jnp.int32),
             buffer(MATS, COLS, ROWS, LANES),
             buffer(MATS, COLS, ROWS, LANES),
             buffer(MATS, COLS, ROWS, LANES),
@@ -256,6 +260,7 @@
             buffer(R // 16, COLS, QUAD, ROWS, LANES),
             buffer(R, C),
             dma((2, 2 * CHUNKS)),
+            dma(()),
             dma(()),
             dma(()),
             dma(()),
@@ -272,13 +277,16 @@
 
 
 def body(grad, momentum, owners):
+    def in_hbm(a):
+        return pltpu.with_memory_space_constraint(a, pltpu.MemorySpace.HBM)
+
     def blocks(a):
         return a.reshape(MATS, ROWS, COLS, LANES).transpose(0, 2, 1, 3)
 
     def rows(a):
         return a.transpose(0, 2, 1, 3).reshape(MATS, ROWS, C)
 
-    new_momentum, update = step(blocks(grad), blocks(momentum), owners.transpose(0, 2, 1))
+    new_momentum, update = step(in_hbm(blocks(grad)), in_hbm(blocks(momentum)), in_hbm(owners.transpose(0, 2, 1)))
     return (rows(new_momentum), rows(update))
 
 

time: 102 us -> 94.7 us (0.928)
  local copies, waits for them, and re-layouts: 7.78 us -> 3.33 us
  Pallas kernels: 93.6 us -> 90.6 us
    unnamed x8 -> x2, local copies, waits for them, and re-layouts: 7.78 us -> 3.33 us
    pallas_call x1, Pallas kernels: 93.6 us -> 90.6 us  [step(): pl.pallas_call(kernel, out_shape=(whole(MATS), whole(MATS)), in_specs=[an...]
where the time goes in v4:
time: 94.7 us; the launch traced here: 94.6 us
  Pallas kernels  90.6 us (96%)
  local copies, waits for them, and re-layouts  3.33 us (4%)
    pallas_call x1, Pallas kernels, step(): pl.pallas_call(kernel, out_shape=(whole(MATS), whole(MATS)), in_specs=[an...  90.6 us
    unnamed x2, local copies, waits for them, and re-layouts  3.33 us

profile of v4, /device:TPU:19, one launch (start us, length us, event | category | flops | bytes accessed | tf_op | source)
XLA Modules:
  0.0 94.6 jit_solution(1918136624256617782)
XLA Ops:
  0.6 90.6 %muon_step.1 = (bf16[192,16,4,128]{3,2,1,0:T(4,128)(2,1)S(1)}, bf16[192,16,4,128]{3,2,1,0:T(4,128)(2,1)S(1)}) custom-call(bf16[192,16,4,128]{3,2,1,0:T(4,128)(2,1)} %bitcast.15, bf16[192,16,4,128]{3,2,1,0:T(4,128)(2,1)} %bitcast.16, s32[2,2,128]{2,1,0:T(2,128)} %bitcast.17), custom_call_target="tpu_custom_call" | custom-call | tf_op jit(solution)/shard_map/muon_step/pallas_call | solution.py:248
  91.3 1.7 %copy.7 = bf16[192,4,2048]{2,1,0:T(4,128)(2,1)} copy(bf16[192,4,2048]{2,1,0:T(4,128)(2,1)S(1)} %bitcast.14) | data formatting | bytes 6291456
  92.9 1.7 %copy.8 = bf16[192,4,2048]{2,1,0:T(4,128)(2,1)} copy(bf16[192,4,2048]{2,1,0:T(4,128)(2,1)S(1)} %bitcast.13) | data formatting | bytes 6291456

commit v5 on v3

v5 whole, which is shorter than its diff:
```python
import functools
import math

import jax
import jax.numpy as jnp
from jax import lax
from jax.experimental import pallas as pl
from jax.experimental.pallas import tpu as pltpu
from jax.sharding import PartitionSpec as P

R = 512
C = 2048
ITERS = 3
MATS = 192

NX, NZ, NY = 4, 8, 4
CHIPS = NX * NZ * NY
PER_REP = MATS // 2
THIRDS = 3
LANES = 128
COLS = C // LANES
ROWS = R // CHIPS
QUAD = 16 // ROWS
CHUNKS = 4
CHUNK = PER_REP // CHUNKS

coef_a = 3.4445
coef_b = -4.775
coef_c = 2.0315
mom_decay = 0.95
out_scale = 0.2 * math.sqrt(max(R, C))


def line_phase(line, rep):
    return (line // NZ + line % NZ + 2 * rep) % NY


def phase(chip, rep):
    return (line_phase(chip // NY, rep) + chip % NY) % NY


def first_z(x, third, rep):
    return x + 4 * rep


def place_in_third(line, third, rep, depth):
    x, z = line // NZ, line % NZ
    rank = (z + 8 * NZ - first_z(x, third, rep)) % NZ
    return jnp.where(rank < depth, x * depth + rank, NX * NZ)


def owner_of(third, place, rep, depth):
    x = place // depth
    line = x * NZ + (place % depth + first_z(x, third, rep)) % NZ
    return line * NY + (third + 1 + NY - line_phase(line, rep)) % NY


def dot(a, b, contract_b):
    return lax.dot_general(a, b, (((1,), (contract_b,)), ((), ())), preferred_element_type=jnp.float32)


def tile(row, col):
    return pl.ds(pl.multiple_of(row * 16, 16), 16), slice(col * LANES, (col + 1) * LANES)


def kernel(
    depth, order, grad, momentum, fresh_out, update,
    gbuf, mbuf, fbuf, nbuf, xbuf, ybuf, xs,
    load_sem, store_sem, send1, recv1, send2, recv2, send3, recv3,
):
    me = lax.axis_index("shard")
    rep = lax.axis_index("rep")
    lines = NX * depth
    used = THIRDS * lines
    turn_of_me = phase(me, rep)
    my_third = (turn_of_me + NY - 1) % NY
    my_place = place_in_third(me // NY, my_third, rep, depth)
    active = jnp.logical_and(turn_of_me != 0, my_place < lines)
    my_slot = lines * my_third + my_place
    mine = PER_REP * rep + my_slot

    barrier = pltpu.get_barrier_semaphore()

    def load(part):
        where = pl.ds(part * CHUNK, CHUNK)
        return (
            pltpu.make_async_copy(grad.at[where], gbuf.at[where], load_sem.at[0, part]),
            pltpu.make_async_copy(momentum.at[where], mbuf.at[where], load_sem.at[1, part]),
        )

    def start_load(part, _):
        for copy in load(part):
            copy.start()
        return 0

    lax.fori_loop(0, 2 * CHUNKS, start_load, 0)

    def greet(k, _):
        pl.semaphore_signal(barrier, 1, device_id={"shard": (me + k) % CHIPS})
        return 0

    lax.fori_loop(1, CHIPS, greet, 0)
    pl.semaphore_signal(barrier, 1, device_id={"rep": 1 - rep})

    def end_load(part, _):
        for copy in load(part):
            copy.wait()
        return 0

    lax.fori_loop(0, 2 * CHUNKS, end_load, 0)

    def fresh_of(matrix, j):
        g = gbuf[matrix, j : j + QUAD].reshape(16, LANES).astype(jnp.float32)
        m = mbuf[matrix, j : j + QUAD].reshape(16, LANES).astype(jnp.float32)
        return g, mom_decay * m + g

    def look_ahead(slot, _):
        matrix = order[PER_REP * rep + slot]
        for j in range(0, COLS, QUAD):
            g, fresh = fresh_of(matrix, j)
            nesterov = (g + mom_decay * fresh).astype(jnp.bfloat16)
            nbuf[slot, j : j + QUAD] = nesterov.reshape(QUAD, ROWS, LANES)
        return 0

    lax.fori_loop(0, used, look_ahead, 0)
    pl.semaphore_wait(barrier, CHIPS)

    def spread(k, _):
        third = k // lines
        place = (13 * (k % lines) + me // NY) % lines
        dst = owner_of(third, place, rep, depth)

        @pl.when(dst != me)
        def _():
            pltpu.make_async_remote_copy(
                nbuf.at[lines * third + place],
                xbuf.at[me // QUAD, :, me % QUAD],
                send1,
                recv1,
                device_id={"shard": dst},
            ).start()

        return 0

    lax.fori_loop(0, used, spread, 0)

    @pl.when(active)
    def _():
        pltpu.make_async_copy(
            nbuf.at[my_slot], xbuf.at[me // QUAD, :, me % QUAD], recv1
        ).start()

    def renew(matrix, _):
        for j in range(0, COLS, QUAD):
            fresh = fresh_of(matrix, j)[1]
            fbuf[matrix, j : j + QUAD] = fresh.astype(jnp.bfloat16).reshape(QUAD, ROWS, LANES)
        return 0

    lax.fori_loop(0, MATS, renew, 0)
    store = pltpu.make_async_copy(fbuf, fresh_out, store_sem)
    store.start()

    @pl.when(active)
    def _():
        pltpu.make_async_copy(xbuf, xbuf, recv1).wait()

        def gather(row, total):
            for col in range(COLS):
                part = xbuf[row, col].reshape(16, LANES)
                rows, lanes = tile(row, col)
                xs[rows, lanes] = part
                wide = part.astype(jnp.float32)
                total = total + wide * wide
            return total

        total = lax.fori_loop(0, R // 16, gather, jnp.zeros((16, LANES), jnp.float32))
        inverse = 1.0 / (jnp.sqrt(jnp.sum(total)) + 1e-07)
        current = (xs[...].astype(jnp.float32) * inverse).astype(jnp.bfloat16)
        for turn in range(ITERS):
            gram = dot(current, current, 1).astype(jnp.bfloat16)
            mixer = (coef_b * gram.astype(jnp.float32) + coef_c * dot(gram, gram, 0)).astype(jnp.bfloat16)
            result = coef_a * current.astype(jnp.float32) + dot(mixer, current, 0)
            if turn + 1 < ITERS:
                current = result.astype(jnp.bfloat16)
            else:
                xs[...] = (out_scale * result).astype(jnp.bfloat16)

        def scatter(row, _):
            for col in range(COLS):
                rows, lanes = tile(row, col)
                ybuf[row, col] = xs[rows, lanes].reshape(QUAD, ROWS, LANES)
            return 0

        lax.fori_loop(0, R // 16, scatter, 0)

        def back(k, _):
            x, z, y = me // (NZ * NY), me // NY % NZ, me % NY
            dst = 37 * k % CHIPS

            @pl.when(dst != me)
            def _():
                pltpu.make_async_remote_copy(
                    ybuf.at[dst // QUAD, :, dst % QUAD],
                    update.at[mine],
                    send2,
                    recv2.at[my_third],
                    device_id={"shard": dst},
                ).start()

            return 0

        lax.fori_loop(0, CHIPS, back, 0)
        pltpu.make_async_copy(
            ybuf.at[me // QUAD, :, me % QUAD], update.at[mine], recv2.at[my_third]
        ).start()

    def third_of(part):
        return update.at[pl.ds(PER_REP * rep + lines * part, lines)]

    def forward(part, _):
        pltpu.make_async_copy(third_of(part), third_of(part), recv2.at[part]).wait()
        pltpu.make_async_remote_copy(
            third_of(part), third_of(part), send3.at[part], recv3.at[part], device_id={"rep": 1 - rep}
        ).start()
        return 0

    lax.fori_loop(0, THIRDS, forward, 0)

    def finish(part, _):
        pltpu.make_async_copy(third_of(part), third_of(part), send3.at[part]).wait()
        pltpu.make_async_copy(third_of(part), third_of(part), recv3.at[part]).wait()
        return 0

    lax.fori_loop(0, THIRDS, finish, 0)
    store.wait()

    @pl.when(active)
    def _():
        most = nbuf.at[pl.ds(0, used - 1)]
        pltpu.make_async_copy(most, most, send1).wait()
        rest = update.at[pl.ds(0, CHIPS - 1)]
        pltpu.make_async_copy(rest, rest, send2).wait()

    @pl.when(jnp.logical_not(active))
    def _():
        full = nbuf.at[pl.ds(0, used)]
        pltpu.make_async_copy(full, full, send1).wait()


def whole(count):
    return jax.ShapeDtypeStruct((count, COLS, ROWS, LANES), jnp.bfloat16)


def buffer(*shape):
    return pltpu.VMEM(shape, jnp.bfloat16)


def put_out(where, fresh, packed, fresh_out, update, zeros, sem):
    zeros[...] = jnp.zeros_like(zeros)
    pltpu.make_async_copy(fresh, fresh_out, sem.at[0]).start()

    def one(matrix, _):
        slot = where[matrix]

        @pl.when(slot >= 0)
        def _():
            pltpu.make_async_copy(packed.at[jnp.maximum(slot, 0)], update.at[matrix], sem.at[1]).start()

        @pl.when(slot < 0)
        def _():
            pltpu.make_async_copy(zeros, update.at[matrix], sem.at[1]).start()

        return 0

    lax.fori_loop(0, MATS, one, 0)
    pltpu.make_async_copy(fresh, fresh_out, sem.at[0]).wait()
    pltpu.make_async_copy(fresh, update, sem.at[1]).wait()


def step(depth, grad, momentum, order, where):
    dma = pltpu.SemaphoreType.DMA
    anywhere = pl.BlockSpec(memory_space=pl.ANY)
    scalars = pl.BlockSpec(memory_space=pltpu.SMEM)
    fresh, packed = pl.pallas_call(
        functools.partial(kernel, depth),
        out_shape=(whole(MATS), whole(MATS)),
        in_specs=[scalars, anywhere, anywhere],
        out_specs=(anywhere, anywhere),
        scratch_shapes=[
            buffer(MATS, COLS, ROWS, LANES),
            buffer(MATS, COLS, ROWS, LANES),
            buffer(MATS, COLS, ROWS, LANES),
            buffer(PER_REP, COLS, ROWS, LANES),
            buffer(R // 16, COLS, QUAD, ROWS, LANES),
            buffer(R // 16, COLS, QUAD, ROWS, LANES),
            buffer(R, C),
            dma((2, 2 * CHUNKS)),
            dma(()),
            dma(()),
            dma(()),
            dma(()),
            dma((THIRDS,)),
            dma((THIRDS,)),
            dma((THIRDS,)),
        ],
        name=f"muon_step_{depth}",
        compiler_params=pltpu.CompilerParams(
            collective_id=depth, has_side_effects=True, vmem_limit_bytes=40 * 1024 * 1024
        ),
    )(order, grad, momentum)
    return pl.pallas_call(
        put_out,
        out_shape=(whole(MATS), whole(MATS)),
        in_specs=[scalars, anywhere, anywhere],
        out_specs=(anywhere, anywhere),
        scratch_shapes=[buffer(COLS, ROWS, LANES), dma((2,))],
        name=f"put_out_{depth}",
        compiler_params=pltpu.CompilerParams(vmem_limit_bytes=1024 * 1024),
    )(where, fresh, packed)


DEPTHS = (7, NZ)


def body(grad, momentum, owners):
    def in_hbm(a):
        return pltpu.with_memory_space_constraint(a, pltpu.MemorySpace.HBM)

    def blocks(a):
        return in_hbm(a.reshape(MATS, ROWS, COLS, LANES).transpose(0, 2, 1, 3))

    def rows(a):
        return a.transpose(0, 2, 1, 3).reshape(MATS, ROWS, C)

    index = jnp.arange(MATS, dtype=jnp.int32)
    table = owners.transpose(0, 2, 1).reshape(4, CHIPS)
    listed = jnp.any(table[:, :, None] == index, axis=(0, 1))
    before = jnp.sum((listed[:, None] & (index[:, None] < index[None, :])).astype(jnp.int32), axis=0)
    few = jnp.sum(listed.astype(jnp.int32)) <= 2 * THIRDS * NX * DEPTHS[0]
    used = jnp.where(few, THIRDS * NX * DEPTHS[0], PER_REP)
    where = jnp.where(listed, jnp.where(before < used, before, PER_REP + before - used), -1)
    order = jnp.sum(jnp.where(where[:, None] == index[None, :], index[:, None], 0), axis=0)
    new_momentum, update = lax.cond(
        few,
        functools.partial(step, DEPTHS[0]),
        functools.partial(step, DEPTHS[1]),
        blocks(grad), blocks(momentum), order, where,
    )
    return (rows(new_momentum), rows(update))


def solution(mesh):
    placed = (P(None, "shard", None), P(None, "shard", None), P())
    return jax.shard_map(
        body,
        mesh=mesh,
        in_specs=placed,
        out_specs=(P(None, "shard", None), P(None, "shard", None)),
        check_vma=False,
    )
```

time: 102 us -> 93.3 us (0.915)
  local copies, waits for them, and re-layouts: 7.78 us -> 0 us
  Pallas kernels: 93.6 us -> 89.4 us
  other arithmetic: 0 us -> 1.67 us
    unnamed x8 -> x0, local copies, waits for them, and re-layouts: 7.78 us -> none
    pallas_call x1 -> x2, Pallas kernels: 93.6 us -> 89.4 us  [the longest x1 86.3 us: step(): pl.pallas_call(functools.partial(kernel, depth), out_shape=(whole(MATS),...]
where the time goes in v5:
time: 93.3 us; the launch traced here: 92.8 us
  Pallas kernels  89.4 us (96%)
  other arithmetic  1.67 us (2%)
  between operations  1.48 us (2%)
    pallas_call x1, Pallas kernels, step(): pl.pallas_call(functools.partial(kernel, depth), out_shape=(whole(MATS),...  86.3 us
    pallas_call x1, Pallas kernels, step(): pl.pallas_call(put_out, out_shape=(whole(MATS), whole(MATS)), in_specs=[s...  3.15 us

profile of v5, /device:TPU:19, one launch (start us, length us, event | category | flops | bytes accessed | tf_op | source)
XLA Modules:
  0.0 92.8 jit_solution(10198990157996249130)
XLA Ops:
  0.6 0.8 fusion
  1.4 0.6 convert_reduce_fusion.1
  2.7 0.1 convert_reduce_fusion
  2.9 0.1 select_reduce_fusion
  3.0 89.7 %conditional.1 = ((bf16[192,16,4,128]{3,2,1,0:T(4,128)(2,1)}, bf16[192,16,4,128]{3,2,1,0:T(4,128)(2,1)})) conditional(s32[]{:T(128)} %convert_element_type.10, (s32[192]{0:T(256)S(1)}, bf16[192,16,4,128]{3,2,1,0:T(4,128)(2,1)}, bf16[192,16,4,128]{3,2,1,0:T(4,128)(2,1)}, s32[192]{0:T(256)S(1)}) %tuple.22, (s32[192]{0:T(256)S(1)}, ...), branch_computations={%region_4.5_spmd, %region_5.6_spmd} | conditional | bytes 8 | solution.py:343
  3.0 86.3 %muon_step_7.1 = (bf16[192,16,4,128]{3,2,1,0:T(4,128)(2,1)S(1)}, bf16[192,16,4,128]{3,2,1,0:T(4,128)(2,1)S(1)}) custom-call(s32[192]{0:T(256)S(1)} %get-tuple-element.23.order, bf16[192,16,4,128]{3,2,1,0:T(4,128)(2,1)} %get-tuple-element.24.grad, bf16[192,16,4,128]{3,2,1,0:T(4,128)(2,1)} %get-tuple-element.25.momentum), custom_call_target="tpu_custom_call" | custom-call | tf_op jit(solution)/shard_map/cond/branch_1_fun/muon_step_7/pallas_call | solution.py:284
  89.3 3.1 %put_out_7.1 = (bf16[192,16,4,128]{3,2,1,0:T(4,128)(2,1)}, bf16[192,16,4,128]{3,2,1,0:T(4,128)(2,1)}) custom-call(s32[192]{0:T(256)S(1)} %get-tuple-element.22.where, bf16[192,16,4,128]{3,2,1,0:T(4,128)(2,1)S(1)} %get-tuple-element.26.fresh, bf16[192,16,4,128]{3,2,1,0:T(4,128)(2,1)S(1)} %get-tuple-element.27.packed), custom_call_target="tpu_custom_call" | custom-call | tf_op jit(solution)/shard_map/cond/branch_1_fun/put_out_7/pallas_call | solution.py:311
  (1 shorter events, 0.0 us)

commit v6 on v5

--- a/solution.py
+++ b/solution.py
@@ -53,6 +53,14 @@
     x = place // depth
     line = x * NZ + (place % depth + first_z(x, third, rep)) % NZ
     return line * NY + (third + 1 + NY - line_phase(line, rep)) % NY
+
+
+def hops(chip):
+    at = (chip // (NZ * NY), chip // NY % NZ, chip % NY)
+    return sum(min(a, n - a) for a, n in zip(at, (NX, NZ, NY)))
+
+
+NEAR_FIRST = sorted((37 * k % CHIPS for k in range(CHIPS)), key=hops)
 
 
 def dot(a, b, contract_b):
@@ -193,10 +201,7 @@
 
         lax.fori_loop(0, R // 16, scatter, 0)
 
-        def back(k, _):
-            x, z, y = me // (NZ * NY), me // NY % NZ, me % NY
-            dst = 37 * k % CHIPS
-
+        def back(dst):
             @pl.when(dst != me)
             def _():
                 pltpu.make_async_remote_copy(
@@ -207,9 +212,9 @@
                     device_id={"shard": dst},
                 ).start()
 
-            return 0
-
-        lax.fori_loop(0, CHIPS, back, 0)
+        for dst in NEAR_FIRST:
+            back(dst)
+
         pltpu.make_async_copy(
             ybuf.at[me // QUAD, :, me % QUAD], update.at[mine], recv2.at[my_third]
         ).start()

time: 93.3 us -> 91.1 us (0.976)
  the two profiles are of different devices: /device:TPU:19 before, /device:TPU:83 now
where the time goes in v6:
time: 91.1 us; the launch traced here: 91 us
  Pallas kernels  87.6 us (96%)
  other arithmetic  1.67 us (2%)
  between operations  1.48 us (2%)
    pallas_call x1, Pallas kernels, step(): pl.pallas_call(functools.partial(kernel, depth), out_shape=(whole(MATS),...  84.4 us
    pallas_call x1, Pallas kernels, step(): pl.pallas_call(put_out, out_shape=(whole(MATS), whole(MATS)), in_specs=[s...  3.15 us

profile of v6, /device:TPU:83, one launch (start us, length us, event | category | flops | bytes accessed | tf_op | source)
XLA Modules:
  0.0 91.0 jit_solution(7750939386266222840)
XLA Ops:
  0.6 0.8 fusion
  1.4 0.6 convert_reduce_fusion.1
  2.7 0.1 convert_reduce_fusion
  2.9 0.1 select_reduce_fusion
  3.0 87.8 %conditional.1 = ((bf16[192,16,4,128]{3,2,1,0:T(4,128)(2,1)}, bf16[192,16,4,128]{3,2,1,0:T(4,128)(2,1)})) conditional(s32[]{:T(128)} %convert_element_type.10, (s32[192]{0:T(256)S(1)}, bf16[192,16,4,128]{3,2,1,0:T(4,128)(2,1)}, bf16[192,16,4,128]{3,2,1,0:T(4,128)(2,1)}, s32[192]{0:T(256)S(1)}) %tuple.22, (s32[192]{0:T(256)S(1)}, ...), branch_computations={%region_4.5_spmd, %region_5.6_spmd} | conditional | bytes 8 | solution.py:348
  3.0 84.4 %muon_step_7.1 = (bf16[192,16,4,128]{3,2,1,0:T(4,128)(2,1)S(1)}, bf16[192,16,4,128]{3,2,1,0:T(4,128)(2,1)S(1)}) custom-call(s32[192]{0:T(256)S(1)} %get-tuple-element.23.order, bf16[192,16,4,128]{3,2,1,0:T(4,128)(2,1)} %get-tuple-element.24.grad, bf16[192,16,4,128]{3,2,1,0:T(4,128)(2,1)} %get-tuple-element.25.momentum), custom_call_target="tpu_custom_call" | custom-call | tf_op jit(solution)/shard_map/cond/branch_1_fun/muon_step_7/pallas_call | solution.py:289
  87.4 3.1 %put_out_7.1 = (bf16[192,16,4,128]{3,2,1,0:T(4,128)(2,1)}, bf16[192,16,4,128]{3,2,1,0:T(4,128)(2,1)}) custom-call(s32[192]{0:T(256)S(1)} %get-tuple-element.22.where, bf16[192,16,4,128]{3,2,1,0:T(4,128)(2,1)S(1)} %get-tuple-element.26.fresh, bf16[192,16,4,128]{3,2,1,0:T(4,128)(2,1)S(1)} %get-tuple-element.27.packed), custom_call_target="tpu_custom_call" | custom-call | tf_op jit(solution)/shard_map/cond/branch_1_fun/put_out_7/pallas_call | solution.py:316
  (1 shorter events, 0.0 us)

commit v7 on v6

--- a/solution.py
+++ b/solution.py
@@ -341,7 +341,7 @@
     table = owners.transpose(0, 2, 1).reshape(4, CHIPS)
     listed = jnp.any(table[:, :, None] == index, axis=(0, 1))
     before = jnp.sum((listed[:, None] & (index[:, None] < index[None, :])).astype(jnp.int32), axis=0)
-    few = jnp.sum(listed.astype(jnp.int32)) <= 2 * THIRDS * NX * DEPTHS[0]
+    few = jnp.sum((table < MATS).astype(jnp.int32)) <= 2 * THIRDS * NX * DEPTHS[0]
     used = jnp.where(few, THIRDS * NX * DEPTHS[0], PER_REP)
     where = jnp.where(listed, jnp.where(before < used, before, PER_REP + before - used), -1)
     order = jnp.sum(jnp.where(where[:, None] == index[None, :], index[:, None], 0), axis=0)

time: 91.1 us -> 91.8 us (level)
  no operation moved by 1% of the time
where the time goes in v7:
time: 91.8 us; the launch traced here: 91.7 us
  Pallas kernels  87.6 us (95%)
  other arithmetic  2.36 us (3%)
  between operations  1.48 us (2%)
    pallas_call x1, Pallas kernels, step(): pl.pallas_call(functools.partial(kernel, depth), out_shape=(whole(MATS),...  84.4 us
    pallas_call x1, Pallas kernels, step(): pl.pallas_call(put_out, out_shape=(whole(MATS), whole(MATS)), in_specs=[s...  3.15 us

profile of v7, /device:TPU:83, one launch (start us, length us, event | category | flops | bytes accessed | tf_op | source)
XLA Modules:
  0.0 91.7 jit_solution(1864440797417465034)
XLA Ops:
  0.6 1.3 %fusion.2 = s32[]{:T(128)} fusion(s32[2,128,2]{1,2,0:T(2,128)} %param.7), kind=kLoop, calls=%fused_computation.9 | loop fusion | flops 1535 | bytes 2052 | tf_op jit(solution)/shard_map/reduce_sum | solution.py:344
  2.6 0.8 fusion
  3.4 0.1 convert_reduce_fusion
  3.5 0.1 select_reduce_fusion
  3.7 87.8 %conditional.1 = ((bf16[192,16,4,128]{3,2,1,0:T(4,128)(2,1)}, bf16[192,16,4,128]{3,2,1,0:T(4,128)(2,1)})) conditional(s32[]{:T(128)} %convert_element_type.11, (s32[192]{0:T(256)S(1)}, bf16[192,16,4,128]{3,2,1,0:T(4,128)(2,1)}, bf16[192,16,4,128]{3,2,1,0:T(4,128)(2,1)}, s32[192]{0:T(256)S(1)}) %tuple.22, (s32[192]{0:T(256)S(1)}, ...), branch_computations={%region_4.5_spmd, %region_5.6_spmd} | conditional | bytes 8 | solution.py:348
  3.7 84.4 %muon_step_7.1 = (bf16[192,16,4,128]{3,2,1,0:T(4,128)(2,1)S(1)}, bf16[192,16,4,128]{3,2,1,0:T(4,128)(2,1)S(1)}) custom-call(s32[192]{0:T(256)S(1)} %get-tuple-element.23.order, bf16[192,16,4,128]{3,2,1,0:T(4,128)(2,1)} %get-tuple-element.24.grad, bf16[192,16,4,128]{3,2,1,0:T(4,128)(2,1)} %get-tuple-element.25.momentum), custom_call_target="tpu_custom_call" | custom-call | tf_op jit(solution)/shard_map/cond/branch_1_fun/muon_step_7/pallas_call | solution.py:289
  88.1 3.1 %put_out_7.1 = (bf16[192,16,4,128]{3,2,1,0:T(4,128)(2,1)}, bf16[192,16,4,128]{3,2,1,0:T(4,128)(2,1)}) custom-call(s32[192]{0:T(256)S(1)} %get-tuple-element.22.where, bf16[192,16,4,128]{3,2,1,0:T(4,128)(2,1)S(1)} %get-tuple-element.26.fresh, bf16[192,16,4,128]{3,2,1,0:T(4,128)(2,1)S(1)} %get-tuple-element.27.packed), custom_call_target="tpu_custom_call" | custom-call | tf_op jit(solution)/shard_map/cond/branch_1_fun/put_out_7/pallas_call | solution.py:316
  (1 shorter events, 0.0 us)

commit v8 on v6

--- a/solution.py
+++ b/solution.py
@@ -101,7 +101,6 @@
             copy.start()
         return 0
 
-    lax.fori_loop(0, 2 * CHUNKS, start_load, 0)
 
     def greet(k, _):
         pl.semaphore_signal(barrier, 1, device_id={"shard": (me + k) % CHIPS})
@@ -109,6 +108,7 @@
 
     lax.fori_loop(1, CHIPS, greet, 0)
     pl.semaphore_signal(barrier, 1, device_id={"rep": 1 - rep})
+    lax.fori_loop(0, 2 * CHUNKS, start_load, 0)
 
     def end_load(part, _):
         for copy in load(part):

time: 91.1 us -> 93.3 us (1.024)
  the two profiles are of different devices: /device:TPU:83 before, /device:TPU:77 now
where the time goes in v8:
time: 93.3 us; the launch traced here: 93.2 us
  Pallas kernels  89.8 us (96%)
  other arithmetic  1.67 us (2%)
  between operations  1.48 us (2%)
    pallas_call x1, Pallas kernels, step(): pl.pallas_call(functools.partial(kernel, depth), out_shape=(whole(MATS),...  86.7 us
    pallas_call x1, Pallas kernels, step(): pl.pallas_call(put_out, out_shape=(whole(MATS), whole(MATS)), in_specs=[s...  3.15 us

profile of v8, /device:TPU:77, one launch (start us, length us, event | category | flops | bytes accessed | tf_op | source)
XLA Modules:
  0.0 93.2 jit_solution(5041210215317162923)
XLA Ops:
  0.6 0.8 fusion
  1.4 0.6 convert_reduce_fusion.1
  2.7 0.1 convert_reduce_fusion
  2.9 0.1 select_reduce_fusion
  3.0 90.1 %conditional.1 = ((bf16[192,16,4,128]{3,2,1,0:T(4,128)(2,1)}, bf16[192,16,4,128]{3,2,1,0:T(4,128)(2,1)})) conditional(s32[]{:T(128)} %convert_element_type.10, (s32[192]{0:T(256)S(1)}, bf16[192,16,4,128]{3,2,1,0:T(4,128)(2,1)}, bf16[192,16,4,128]{3,2,1,0:T(4,128)(2,1)}, s32[192]{0:T(256)S(1)}) %tuple.22, (s32[192]{0:T(256)S(1)}, ...), branch_computations={%region_4.5_spmd, %region_5.6_spmd} | conditional | bytes 8 | solution.py:348
  3.0 86.7 %muon_step_7.1 = (bf16[192,16,4,128]{3,2,1,0:T(4,128)(2,1)S(1)}, bf16[192,16,4,128]{3,2,1,0:T(4,128)(2,1)S(1)}) custom-call(s32[192]{0:T(256)S(1)} %get-tuple-element.23.order, bf16[192,16,4,128]{3,2,1,0:T(4,128)(2,1)} %get-tuple-element.24.grad, bf16[192,16,4,128]{3,2,1,0:T(4,128)(2,1)} %get-tuple-element.25.momentum), custom_call_target="tpu_custom_call" | custom-call | tf_op jit(solution)/shard_map/cond/branch_1_fun/muon_step_7/pallas_call | solution.py:289
  89.7 3.1 %put_out_7.1 = (bf16[192,16,4,128]{3,2,1,0:T(4,128)(2,1)}, bf16[192,16,4,128]{3,2,1,0:T(4,128)(2,1)}) custom-call(s32[192]{0:T(256)S(1)} %get-tuple-element.22.where, bf16[192,16,4,128]{3,2,1,0:T(4,128)(2,1)S(1)} %get-tuple-element.26.fresh, bf16[192,16,4,128]{3,2,1,0:T(4,128)(2,1)S(1)} %get-tuple-element.27.packed), custom_call_target="tpu_custom_call" | custom-call | tf_op jit(solution)/shard_map/cond/branch_1_fun/put_out_7/pallas_call | solution.py:316
  (1 shorter events, 0.0 us)
